TPU v7x, 128 devices: a whole 4x4x4 slice. The times are simulated.
128 devices in a mesh: row: 8 (over y, core), col: 16 (over x, z).
Axes of the slice: x: 4, y: 4, z: 4, core: 2. Of those that a mesh axis runs over, the one named last changes fastest.
Arguments:
- theta: float32 [64, 256, 256], P('row', None, 'col'), may hold values from -6 to 6
- left_env: float32 [32, 32, 256, 256], P('row', 'col'), as said below
- right_env: float32 [8, 32, 256, 256], P(None, 'col'), as said below
- left_sector: int32 [64], replicated, may hold values from 0 to 31, as said below
- right_sector: int32 [64], P('row'), may hold values from 0 to 7
- term_on: int32 [64, 32], P('row', 'col'), may hold values 0 or 1
- left_size: int32 [32], replicated, may hold values from 1 to 256, 5120 in all
- right_size: int32 [8], replicated, may hold values from 1 to 256, 1280 in all
Outputs:
- new_theta: float32 [64, 256, 256], P('row', None, 'col')
- energy: float32 [], replicated
Inputs may be any that keep to these rules, and one draw needn't show every extreme that they name: `left_sector`: left sector s belongs to row s // 4. Block k belongs to row k // 8. The 8 blocks of one row name distinct left sectors; they name either none or exactly 2 sectors belonging to any one row, and the blocks of every row name 2 sectors belonging to one common row. `left_env`: each tile is symmetric in its last two dimensions. `right_env`: each tile is symmetric in its last two dimensions.
All inputs are finite; a program needn't handle non-finite values. No bound on the sum of `term_on` on one device may be relied on, other than what follows from the above.
Results may differ from a plain program's by a relative error of at most 0.0001.
Values sent between devices are 32-bit elements; how exact they have to be, the bound alone decides.
No kernel may reach another device: no remote copies, remote signals or barrier semaphores. Data moves between devices by JAX's collectives and lax.ppermute only.
A program may use at most 128 MiB of HBM per device.

v0:
```python
import jax
import jax.numpy as jnp
from jax import lax
from jax.sharding import Mesh, PartitionSpec as P

ITERS = 2
HALF = 128
COL = ("x", "z")
ALL = ("y", "c", "x", "z")
SWAP = [(0, 1), (1, 0)]
high = lax.Precision.HIGH


def grids():
    i = lax.broadcasted_iota(jnp.int32, (HALF, HALF), 0)
    j = lax.broadcasted_iota(jnp.int32, (HALF, HALF), 1)
    return (i, j)


def pack(tiles):
    i, j = grids()
    a00 = tiles[:, :HALF, :HALF]
    a01 = tiles[:, :HALF, HALF:]
    a11 = tiles[:, HALF:, HALF:]
    fold = jnp.where(i >= j, a00, a11)
    diag = jnp.sum(jnp.where(i == j, a11, 0.0), axis=1, keepdims=True)
    extra = jnp.pad(diag, ((0, 0), (0, 7), (0, HALF)))
    return jnp.concatenate([jnp.concatenate([fold, a01], axis=2), extra], axis=1)


def unpack(packed):
    i, j = grids()
    fold = packed[:, :HALF, :HALF]
    a01 = packed[:, :HALF, HALF:]
    diag = packed[:, HALF : HALF + 1, :HALF]
    flip = jnp.swapaxes(fold, 1, 2)
    a00 = jnp.where(i >= j, fold, flip)
    a11 = jnp.where(i == j, diag, jnp.where(i < j, fold, flip))
    top = jnp.concatenate([a00, a01], axis=2)
    low = jnp.concatenate([jnp.swapaxes(a01, 1, 2), a11], axis=2)
    return jnp.concatenate([top, low], axis=1)


def safe_div(value, norm):
    return jnp.where(norm > 0.0, value / jnp.where(norm > 0.0, norm, 1.0), 0.0)


def in_order(core, own, other):
    return jnp.where(core == 0, jnp.concatenate([own, other]), jnp.concatenate([other, own]))


def ritz_pair(stats):
    norm, a1, b1, a2, b2, a3 = [stats[:, m] for m in range(6)]

    def apply(x):
        return jnp.stack(
            [a1 * x[0] + b1 * x[1], b1 * x[0] + a2 * x[1] + b2 * x[2], b2 * x[1] + a3 * x[2]]
        )

    zero = jnp.zeros_like(norm)
    start = jnp.stack([norm, zero, zero])
    image = apply(start)
    norm_sq = jnp.sum(start * start)
    correlation = jnp.sum(start * image)
    inv_norm = 1.0 / jnp.sqrt(norm_sq)
    basis = start * inv_norm
    applied = image * inv_norm
    ritz = correlation / norm_sq
    for _ in range(ITERS):
        residual = applied - ritz * basis
        res_sq = jnp.sum(residual * residual)
        length = jnp.sqrt(res_sq)
        fresh = residual / length
        fresh_applied = apply(fresh)
        curvature = jnp.sum(fresh * fresh_applied)
        half_gap = 0.5 * (ritz - curvature)
        root = jnp.sqrt(half_gap * half_gap + res_sq)
        lowest = 0.5 * (ritz + curvature) - root
        first = curvature - lowest
        pair = jnp.sqrt(first * first + res_sq)
        basis = (first * basis - length * fresh) / pair
        applied = (first * applied - length * fresh_applied) / pair
        ritz = lowest
    return (basis, ritz)


def local(theta, left_env, right_env, left_sector, right_sector, term_on, left_size, right_size):
    plane = lax.axis_index("y")
    core = lax.axis_index("c")
    place = lax.axis_index(COL)
    tile = theta.shape[1]
    blocks = theta.shape[0]
    thin = jnp.swapaxes(theta, 1, 2)
    about = jnp.concatenate([right_sector[:, None], term_on], axis=1)
    about16 = in_order(core, about, lax.ppermute(about, "c", SWAP))
    thin16 = in_order(core, thin, lax.ppermute(thin, "c", SWAP))
    right16 = about16[:, 0]
    on16 = jnp.where(core == 0, about16[:, 1], about16[:, 2]).astype(jnp.float32)
    left16 = lax.dynamic_slice_in_dim(left_sector, plane * 16, 16)
    mine = pack(lax.dynamic_index_in_dim(left_env, core, 1, keepdims=False))
    theirs = pack(lax.dynamic_index_in_dim(left_env, 1 - core, 1, keepdims=False))
    eight = in_order(core, mine, lax.ppermute(theirs, "c", SWAP))
    every = lax.all_gather(eight, "y", axis=0, tiled=True)
    right_term = lax.dynamic_index_in_dim(right_env, core, 1, keepdims=False)
    right_slots = pack(jnp.take(right_term, right16, axis=0) * on16[:, None, None])
    slots = jnp.concatenate([right_slots, thin16], axis=1)
    arrived = lax.all_to_all(slots, COL, 0, 0, tiled=True)
    right = unpack(arrived[:, :136])
    block = arrived[:, 136:].reshape(tile, tile)
    left = unpack(lax.all_to_all(jnp.take(every, left16, axis=0), COL, 0, 0, tiled=True))
    live_left = left_size[left16[place]]
    live_right = right_size[right16[place]]
    at = lax.broadcasted_iota(jnp.int32, (tile, tile), 0)
    along = lax.broadcasted_iota(jnp.int32, (tile, tile), 1)
    mask = ((at < live_right) & (along < live_left)).astype(jnp.float32)

    def half_image(u):
        middle = jnp.einsum("wjb,bi->wji", right, u, precision=high)
        return jnp.einsum("wja,wai->ji", middle, left, precision=high)

    def operate(u):
        part = half_image(u)
        return (part + lax.ppermute(part, "c", SWAP)) * mask

    start = block * mask
    norm = jnp.sqrt(jnp.sum(start * start))
    q1 = safe_div(start, norm)
    h1 = operate(q1)
    a1 = jnp.sum(q1 * h1)
    w1 = h1 - a1 * q1
    w1 = w1 - jnp.sum(q1 * w1) * q1
    b1 = jnp.sqrt(jnp.sum(w1 * w1))
    q2 = safe_div(w1, b1)
    h2 = operate(q2)
    a2 = jnp.sum(q2 * h2)
    w2 = h2 - a2 * q2 - b1 * q1
    w2 = w2 - jnp.sum(q2 * w2) * q2 - jnp.sum(q1 * w2) * q1
    b2 = jnp.sqrt(jnp.sum(w2 * w2))
    q3 = safe_div(w2, b2)
    a3 = jnp.sum(q3 * half_image(q3))
    sent = jnp.where(core == 0, q2, q3).reshape(16, theta.shape[2], tile)
    got = lax.all_to_all(sent, COL, 0, 0, tiled=True)
    keep = lax.dynamic_slice_in_dim(got, core * blocks, blocks)
    give = lax.dynamic_slice_in_dim(got, (1 - core) * blocks, blocks)
    back = lax.ppermute(give, "c", SWAP)
    thin2 = jnp.where(core == 0, keep, back)
    thin3 = jnp.where(core == 0, back, keep)
    zero = jnp.float32(0.0)
    mine_stats = jnp.stack([norm, a1, b1, a2, b2, a3, zero, zero])
    stats = lax.all_to_all(jnp.broadcast_to(mine_stats, (128, 8)), ALL, 0, 0, tiled=True)
    stats = stats.reshape(4, 2, 16, 8)
    both = jnp.concatenate([stats[:, 0, :, :5], stats[:, 0, :, 5:] + stats[:, 1, :, 5:]], axis=2)
    both = both.reshape(64, 8)
    basis, ritz = ritz_pair(both)
    scale = jnp.sqrt(jnp.float32(64 * tile * tile))
    row = plane * 2 + core
    first = safe_div(basis[0], both[:, 0])
    coef = jnp.stack([first, basis[1], basis[2]]) * scale
    coef = lax.dynamic_slice_in_dim(coef, row * blocks, blocks, axis=1)
    own_left = lax.dynamic_slice_in_dim(left16, core * blocks, blocks)
    rows_live = left_size[own_left]
    cols_live = right_size[right_sector]
    cols = place * theta.shape[2] + lax.broadcasted_iota(jnp.int32, thin.shape, 1)
    rows = lax.broadcasted_iota(jnp.int32, thin.shape, 2)
    live = (cols < cols_live[:, None, None]) & (rows < rows_live[:, None, None])
    out = (
        coef[0][:, None, None] * jnp.where(live, thin, 0.0)
        + coef[1][:, None, None] * thin2
        + coef[2][:, None, None] * thin3
    )
    return (jnp.swapaxes(out, 1, 2), ritz)


def solution(mesh):
    fine = Mesh(mesh.devices.reshape(4, 2, 4, 4), ALL)
    row = ("y", "c")
    placed = (
        P(row, None, COL),
        P(row, COL, None, None),
        P(None, COL, None, None),
        P(),
        P(row),
        P(row, COL),
        P(),
        P(),
    )
    return jax.shard_map(
        local, mesh=fine, in_specs=placed, out_specs=(P(row, None, COL), P()), check_vma=False
    )
```

profile of v0, /device:TPU:1, one launch (start us, length us, event | category | flops | bytes accessed | tf_op | source)
XLA Modules:
  0.0 207.7 jit_solution(6810230765719790135)
XLA Ops:
  7.2 1.7 dynamic-slice_bitcast_fusion.1
  9.2 1.5 collective-permute-start.2
  10.7 1.6 collective-permute-done.2
  12.2 1.2 maximum_select_fusion
  14.1 1.8 dynamic-slice_bitcast_fusion
  16.0 2.8 %gather_fusion = f32[16,256,256]{2,1,0:T(8,128)} fusion(f32[8,256,256]{2,1,0:T(8,128)S(1)} %dynamic-slice_bitcast_fusion, s32[1024]{0:T(1024)S(1)} %pad_clamp_fusion.3), kind=kCustom, calls=%fused_computation | custom fusion | bytes 8388672 | tf_op jit(solution)/shard_map/jit(_take)/gather | solution.py:105
  18.8 2.8 %select_multiply_fusion = f32[16,256,256]{2,1,0:T(8,128)S(1)} fusion(f32[16,256,256]{2,1,0:T(8,128)} %gather_fusion, f32[16]{0:T(128)S(1)} %get-tuple-element.64, pred[16]{0:T(512)(128)(4,1)S(1)} %and_bitcast_fusion), kind=kLoop, calls=%fused_computation.6 | loop fusion | flops 2097152 | bytes 8388688 | tf_op jit(solution)/shard_map/mul | solution.py:105
  21.9 1.7 fusion
  23.6 7.7 %all-to-all-start = ((f32[16,152,256]{2,1,0:T(8,128)}), f32[16,152,256]{2,1,0:T(8,128)S(1)}, u32[]{:S(2)}, u32[]{:S(2)}) async-start(f32[16,152,256]{2,1,0:T(8,128)} %fusion), calls=%async_computation | async-start | bytes 4980736 | tf_op jit(solution)/shard_map/all_to_all | solution.py:107
  31.4 34.8 %all-gather.2.cloned.1.call-done = f32[32,136,256]{2,1,0:T(8,128)} async-done(((f32[8,136,256]{2,1,0:T(8,128)}), f32[32,136,256]{2,1,0:T(8,128)}) %all-gather.2.cloned.1.call-update) | async-done | bytes 4456464 | tf_op jit(solution)/shard_map/all_gather | solution.py:103
  66.2 4.4 %gather_fusion.1 = f32[16,136,256]{2,1,0:T(8,128)} fusion(f32[32,136,256]{2,1,0:T(8,128)} %all-gather.2.cloned.1.call-done, s32[1024]{0:T(1024)S(1)} %pad_clamp_fusion.2), kind=kCustom, calls=%fused_computation.1 | custom fusion | bytes 4456512 | tf_op jit(solution)/shard_map/jit(_take)/gather | solution.py:110
  70.6 3.3 %broadcast_select_fusion = f32[16,136,256]{2,1,0:T(8,128)} fusion(f32[16,136,256]{2,1,0:T(8,128)} %gather_fusion.1, pred[16]{0:T(512)(128)(4,1)S(1)} %get-tuple-element.20), kind=kLoop, calls=%fused_computation.18 | loop fusion | flops 557056 | bytes 4456464 | tf_op jit(solution)/shard_map/jit(_take)/select_n | solution.py:110
  74.0 6.7 %all-to-all-start.1 = ((f32[16,136,256]{2,1,0:T(8,128)}), f32[16,136,256]{2,1,0:T(8,128)}, u32[]{:S(2)}, u32[]{:S(2)}) async-start(f32[16,136,256]{2,1,0:T(8,128)} %broadcast_select_fusion), calls=%async_computation.1 | async-start | bytes 4456448 | tf_op jit(solution)/shard_map/all_to_all | solution.py:110
  87.0 1.3 iota_compare_fusion.7
  88.9 0.7 multiply_reduce_fusion.7
  90.4 1.1 slice.189
  91.5 2.5 %copy.54 = f32[16,128,128]{1,2,0:T(8,128)} copy(f32[16,128,128]{2,1,0:T(8,128)} %slice.189) | data formatting | bytes 2097152 | tf_op jit(solution)/shard_map/slice | solution.py:33
  94.1 16.2 %all-to-all-done.1 = f32[16,136,256]{2,1,0:T(8,128)} async-done(((f32[16,136,256]{2,1,0:T(8,128)}), f32[16,136,256]{2,1,0:T(8,128)}, u32[]{:S(2)}, u32[]{:S(2)}) %all-to-all-start.1) | async-done | bytes 2228256 | tf_op jit(solution)/shard_map/all_to_all | solution.py:110
  110.3 2.3 %slice.198 = f32[16,128,128]{2,1,0:T(8,128)} slice(f32[16,136,256]{2,1,0:T(8,128)} %all-to-all-done.1), slice={[0:16], [0:128], [0:128]} | slice | bytes 2097152 | tf_op jit(solution)/shard_map/slice | solution.py:33
  112.7 2.6 %copy.66 = f32[16,128,128]{1,2,0:T(8,128)} copy(f32[16,128,128]{2,1,0:T(8,128)} %slice.198) | data formatting | bytes 2097152
  115.3 0.8 slice.200
  116.1 5.4 %bitcast_select_fusion.1 = (f32[16,128,128]{2,1,0:T(8,128)}, f32[16,128,128]{2,1,0:T(8,128)}, f32[16,128,128]{2,1,0:T(8,128)}, f32[16,128,128]{2,1,0:T(8,128)}, ...) fusion(f32[16,128,128]{1,2,0:T(8,128)} %copy.66, ...), kind=kLoop, calls=%fused_computation.21 | loop fusion | flops 1572864 | bytes 13697024 | tf_op jit(solution)/shard_map/jit(_where)/select_n | solution.py:37
  121.5 1.6 copy.56
  123.1 2.5 %copy.67 = f32[16,128,128]{1,2,0:T(8,128)} copy(f32[16,128,128]{2,1,0:T(8,128)} %get-tuple-element.33) | data formatting | bytes 2097152
  125.7 3.6 %fusion.7 = f32[16,256,256]{2,1,0:T(8,128)S(1)} fusion(f32[16,128,128]{2,1,0:T(8,128)} %get-tuple-element.46, f32[16,128,128]{2,1,0:T(8,128)S(1)} %copy.56, f32[16,128,128]{2,1,0:T(8,128)S(1)} %copy-done.2, f32[16,128,128]{2,1,0:T(8,128)} %get-tuple-element.47, f32[256,256]{1,0:T(8,128)S(1)} %fusion.10), kind=kOutput, calls=%fused_computation.31 | convolution fusion | flops 1613758464 | bytes 8650752 | tf_op jit(solution)/shard_map/wjb,bi->wji/dot_general | solution.py:118
  129.4 2.2 %convolution_bitcast_fusion.2 = f32[256,256]{1,0:T(8,128)S(1)} fusion(f32[16,256,256]{2,1,0:T(8,128)S(1)} %fusion.7, f32[16,128,128]{2,1,0:T(8,128)S(1)} %copy-done.12, f32[16,128,128]{2,1,0:T(8,128)S(1)} %bitcast.176, f32[16,128,128]{2,1,0:T(8,128)S(1)} %copy-done.3, f32[16,128,128]{2,1,0:T(8,128)S(1)} %copy-done.9), kind=kOutput, calls=%fused_computation.15 | convolution fusion | flops 1613758464 | bytes 8650752 | tf_op jit(solution)/shard_map/wja,wai->ji/dot_general | solution.py:119
  131.5 3.6 %collective-permute-start.3 = (f32[256,256]{1,0:T(8,128)S(1)}, f32[256,256]{1,0:T(8,128)S(1)}, u32[]{:S(2)}, u32[]{:S(2)}) collective-permute-start(f32[256,256]{1,0:T(8,128)S(1)} %convolution_bitcast_fusion.2), channel_id=1, source_target_pairs={{0,16},{16,0},{1,17},{17,1},{2,18},{18,2},{3,19},{19,3},{4,20},{20... | collective-permute-start | bytes 786440 | tf_op jit(solution)/shard_map/ppermute | solution.py:123
  135.2 1.1 collective-permute-done.3
  136.3 0.8 multiply_reduce_fusion.6
  137.1 1.4 multiply_reduce_fusion.5
  138.5 2.0 multiply_reduce_fusion.4
  141.3 1.4 divide_select_fusion.1
  142.7 3.6 %fusion.6 = f32[16,256,256]{2,1,0:T(8,128)S(1)} fusion(f32[16,128,128]{2,1,0:T(8,128)} %get-tuple-element.46, f32[16,128,128]{2,1,0:T(8,128)S(1)} %copy.56, f32[16,128,128]{2,1,0:T(8,128)S(1)} %copy-done.2, f32[16,128,128]{2,1,0:T(8,128)} %get-tuple-element.47, f32[256,256]{1,0:T(8,128)S(1)} %divide_select_fusion.1), kind=kOutput, calls=%fused_computation.30 | convolution fusion | flops 1613758464 | bytes 8650752 | tf_op jit(solution)/shard_map/wjb,bi->wji/dot_general | solution.py:118
  146.4 2.2 %convolution_bitcast_fusion.1 = f32[256,256]{1,0:T(8,128)S(1)} fusion(f32[16,256,256]{2,1,0:T(8,128)S(1)} %fusion.6, f32[16,128,128]{2,1,0:T(8,128)S(1)} %copy-done.13, f32[16,128,128]{2,1,0:T(8,128)S(1)} %bitcast.177, f32[16,128,128]{2,1,0:T(8,128)S(1)} %copy-done.4, f32[16,128,128]{2,1,0:T(8,128)S(1)} %copy-done.10), kind=kOutput, calls=%fused_computation.14 | convolution fusion | flops 1613758464 | bytes 8650752 | tf_op jit(solution)/shard_map/wja,wai->ji/dot_general | solution.py:119
  150.3 0.7 multiply_reduce_fusion.3
  151.1 1.4 multiply_reduce_fusion.2
  152.5 2.7 %multiply_reduce_fusion = (f32[]{:T(128)}, f32[256,256]{1,0:T(8,128)S(1)}) fusion(f32[]{:T(128)} %get-tuple-element.7, f32[256,256]{1,0:T(8,128)S(1)} %divide_select_fusion.1, f32[]{:T(128)} %get-tuple-element.6, f32[]{:T(128)} %sqrt.31, f32[256,256]{1,0:T(8,128)S(1)} %get-tuple-element.17, f32[]{:T(128)} %get-tuple-element.16, f32[]{:T(128)S(6)} %select_n.228, ...), kind=kLoop, calls=%fused_computation.47 | loop fusion | flops 917503 | bytes 1049113 | tf_op jit(solution)/shard_map/reduce_sum | solution.py:138
  155.8 3.6 %fusion.5 = f32[16,256,256]{2,1,0:T(8,128)S(1)} fusion(f32[16,128,128]{2,1,0:T(8,128)} %get-tuple-element.46, f32[16,128,128]{2,1,0:T(8,128)S(1)} %copy.56, f32[16,128,128]{2,1,0:T(8,128)S(1)} %copy-done.2, f32[16,128,128]{2,1,0:T(8,128)} %get-tuple-element.47, f32[256,256]{1,0:T(8,128)S(1)} %get-tuple-element.15, f32[]{:T(128)S(6)} %select_n.249, pred[]{:T(512)S(6)} %gt.28), kind=kOutput, calls=%fused_computation.29 | convolution fusion | flops 1613889536 | bytes 8650757 | tf_op jit(solution)/shard_map/wjb,bi->wji/dot_general | solution.py:118
  159.5 2.8 %fusion.8 = f32[]{:T(128)} fusion(f32[16,256,256]{2,1,0:T(8,128)S(1)} %fusion.5, f32[16,128,128]{2,1,0:T(8,128)S(1)} %copy-done.14, f32[16,128,128]{2,1,0:T(8,128)S(1)} %bitcast.178, f32[16,128,128]{2,1,0:T(8,128)S(1)} %copy-done.5, f32[16,128,128]{2,1,0:T(8,128)S(1)} %copy-done.11, f32[256,256]{1,0:T(8,128)S(1)} %get-tuple-element.15, f32[]{:T(128)S(6)} %select_n.249, ...), kind=kOutput, calls=%fused_computation.32 | convolution fusion | flops 1614020608 | bytes 8650761 | tf_op jit(solution)/shard_map/wja,wai->ji/dot_general | solution.py:119
  162.2 1.8 stack.54
  164.1 0.7 broadcast_in_dim.146
  164.7 4.8 %all-to-all-start.2 = ((f32[128,1,8]{2,1,0:T(1,128)}), f32[128,1,8]{2,1,0:T(1,128)S(1)}, u32[]{:S(2)}, u32[]{:S(2)}) async-start(f32[128,1,8]{2,1,0:T(1,128)} %broadcast_in_dim.146), calls=%async_computation.2 | async-start | bytes 131072 | tf_op jit(solution)/shard_map/all_to_all | solution.py:150
  169.6 0.7 broadcast_select_fusion.1
  170.3 8.7 %all-to-all-done.2 = f32[128,1,8]{2,1,0:T(1,128)S(1)} async-done(((f32[128,1,8]{2,1,0:T(1,128)}), f32[128,1,8]{2,1,0:T(1,128)S(1)}, u32[]{:S(2)}, u32[]{:S(2)}) %all-to-all-start.2) | async-done | bytes 4128 | tf_op jit(solution)/shard_map/all_to_all | solution.py:150
  179.0 3.5 %all-to-all-start.3 = ((f32[16,16,256]{2,1,0:T(8,128)}), f32[16,16,256]{2,1,0:T(8,128)S(1)}, u32[]{:S(2)}, u32[]{:S(2)}) async-start(f32[16,16,256]{2,1,0:T(8,128)} %bitcast.44), calls=%async_computation.3 | async-start | bytes 524288 | tf_op jit(solution)/shard_map/all_to_all | solution.py:142
  196.8 1.1 collective-permute-start.5
  197.9 1.0 collective-permute-done.5
  198.9 0.8 add_bitcast_fusion
  (106 shorter events, 10.5 us)
Async XLA Ops:
  7.2 59.1 %all-gather.2.cloned.1.call-start = ((), (), s32[]{:S(2)}) async-start(), calls=%async_computation.4 | async-start | bytes 5570560 | tf_op jit(solution)/shard_map/all_gather | solution.py:103
  8.9 4.5 %copy-start.16 = (s32[8,2]{0,1:T(2,128)S(1)}, s32[8,2]{0,1:T(2,128)}, u32[]{:S(2)}) copy-start(s32[8,2]{0,1:T(2,128)} %param.13) | copy-start | bytes 196
  9.0 4.5 %copy-start.17 = (s32[8]{0:T(128)S(1)}, s32[8]{0:T(128)}, u32[]{:S(2)}) copy-start(s32[8]{0:T(128)} %param.12) | copy-start | bytes 100
  9.0 5.0 %copy-start.15 = (f32[8,256,16]{1,2,0:T(8,128)S(1)}, f32[8,256,16]{1,2,0:T(8,128)}, u32[]{:S(2)}) copy-start(f32[8,256,16]{1,2,0:T(8,128)} %param.8) | copy-start | bytes 393220
  9.2 3.1 %collective-permute-start.2 = (f32[4,136,256]{2,1,0:T(8,128)S(1)}, f32[4,136,256]{2,1,0:T(8,128)S(1)}, u32[]{:S(2)}, u32[]{:S(2)}) collective-permute-start(f32[4,136,256]{2,1,0:T(8,128)S(1)} %select_maximum_fusion.1), channel_id=1, source_target_pairs={{0,16},{16,0},{1,17},{17,1},{2,18},{18,2},{3,19},{19,3},{4,20},{20... | collective-permute-start | bytes 1671176 | tf_op jit(solution)/shard_map/ppermute | solution.py:102
  13.5 2.4 %collective-permute-start = (s32[8,3]{0,1:T(4,128)S(1)}, s32[8,3]{0,1:T(4,128)S(1)}, u32[]{:S(2)}, u32[]{:S(2)}) collective-permute-start(s32[8,3]{0,1:T(4,128)S(1)} %pad_add_fusion), channel_id=1, source_target_pairs={{0,16},{16,0},{1,17},{17,1},{2,18},{18,2},{3,19},{19,3},{4,20},{20... | collective-permute-start | bytes 296 | tf_op jit(solution)/shard_map/ppermute | solution.py:95
  13.9 7.9 %collective-permute-start.1 = (f32[8,16,256]{2,1,0:T(8,128)S(1)}, f32[8,16,256]{2,1,0:T(8,128)S(1)}, u32[]{:S(2)}, u32[]{:S(2)}) collective-permute-start(f32[8,16,256]{2,1,0:T(8,128)S(1)} %bitcast.179), channel_id=1, source_target_pairs={{0,16},{16,0},{1,17},{17,1},{2,18},{18,2},{3,19},{19,3},{4,20},{20... | collective-permute-start | bytes 393224 | tf_op jit(solution)/shard_map/ppermute | solution.py:96
  21.9 9.4 %copy-start.18 = (s32[64]{0:T(128)S(1)}, s32[64]{0:T(128)}, u32[]{:S(2)}) copy-start(s32[64]{0:T(128)} %param.11) | copy-start | bytes 772
  23.6 50.4 %all-to-all-start = ((f32[16,152,256]{2,1,0:T(8,128)}), f32[16,152,256]{2,1,0:T(8,128)S(1)}, u32[]{:S(2)}, u32[]{:S(2)}) async-start(f32[16,152,256]{2,1,0:T(8,128)} %fusion), calls=%async_computation | async-start | bytes 4980736 | tf_op jit(solution)/shard_map/all_to_all | solution.py:107
  70.6 12.6 %copy-start = (s32[32]{0:T(128)S(1)}, s32[32]{0:T(128)}, u32[]{:S(2)}) copy-start(s32[32]{0:T(128)} %param.14) | copy-start | bytes 388
  70.6 15.8 %copy-start.1 = (s32[8]{0:T(128)S(1)}, s32[8]{0:T(128)}, u32[]{:S(2)}) copy-start(s32[8]{0:T(128)} %param.15) | copy-start | bytes 100
  74.0 36.4 %all-to-all-start.1 = ((f32[16,136,256]{2,1,0:T(8,128)}), f32[16,136,256]{2,1,0:T(8,128)}, u32[]{:S(2)}, u32[]{:S(2)}) async-start(f32[16,136,256]{2,1,0:T(8,128)} %broadcast_select_fusion), calls=%async_computation.1 | async-start | bytes 4456448 | tf_op jit(solution)/shard_map/all_to_all | solution.py:110
  121.5 4.2 %copy-start.2 = (f32[16,128,128]{2,1,0:T(8,128)S(1)}, f32[16,128,128]{2,1,0:T(8,128)}, u32[]{:S(2)}) copy-start(f32[16,128,128]{2,1,0:T(8,128)} %get-tuple-element.44) | copy-start | bytes 3145732
  125.7 3.7 %copy-start.3 = (f32[16,128,128]{2,1,0:T(8,128)S(1)}, f32[16,128,128]{2,1,0:T(8,128)}, u32[]{:S(2)}) copy-start(f32[16,128,128]{2,1,0:T(8,128)} %get-tuple-element.33) | copy-start | bytes 3145732
  125.7 3.7 %copy-start.6 = (f32[16,128,128]{1,2,0:T(8,128)S(1)}, f32[16,128,128]{1,2,0:T(8,128)}, u32[]{:S(2)}) copy-start(f32[16,128,128]{1,2,0:T(8,128)} %copy.67) | copy-start | bytes 3145732
  125.7 3.7 %copy-start.9 = (f32[16,128,128]{2,1,0:T(8,128)S(1)}, f32[16,128,128]{2,1,0:T(8,128)}, u32[]{:S(2)}) copy-start(f32[16,128,128]{2,1,0:T(8,128)} %get-tuple-element.27) | copy-start | bytes 3145732
  125.7 3.7 %copy-start.12 = (f32[16,128,128]{2,1,0:T(8,128)S(1)}, f32[16,128,128]{2,1,0:T(8,128)}, u32[]{:S(2)}) copy-start(f32[16,128,128]{2,1,0:T(8,128)} %get-tuple-element.28) | copy-start | bytes 3145732
  131.5 4.8 %collective-permute-start.3 = (f32[256,256]{1,0:T(8,128)S(1)}, f32[256,256]{1,0:T(8,128)S(1)}, u32[]{:S(2)}, u32[]{:S(2)}) collective-permute-start(f32[256,256]{1,0:T(8,128)S(1)} %convolution_bitcast_fusion.2), channel_id=1, source_target_pairs={{0,16},{16,0},{1,17},{17,1},{2,18},{18,2},{3,19},{19,3},{4,20},{20... | collective-permute-start | bytes 786440 | tf_op jit(solution)/shard_map/ppermute | solution.py:123
  142.7 3.7 %copy-start.4 = (f32[16,128,128]{2,1,0:T(8,128)S(1)}, f32[16,128,128]{2,1,0:T(8,128)}, u32[]{:S(2)}) copy-start(f32[16,128,128]{2,1,0:T(8,128)} %get-tuple-element.33) | copy-start | bytes 3145732
  142.7 3.7 %copy-start.7 = (f32[16,128,128]{1,2,0:T(8,128)S(1)}, f32[16,128,128]{1,2,0:T(8,128)}, u32[]{:S(2)}) copy-start(f32[16,128,128]{1,2,0:T(8,128)} %copy.67) | copy-start | bytes 3145732
  142.7 3.7 %copy-start.10 = (f32[16,128,128]{2,1,0:T(8,128)S(1)}, f32[16,128,128]{2,1,0:T(8,128)}, u32[]{:S(2)}) copy-start(f32[16,128,128]{2,1,0:T(8,128)} %get-tuple-element.27) | copy-start | bytes 3145732
  142.7 3.7 %copy-start.13 = (f32[16,128,128]{2,1,0:T(8,128)S(1)}, f32[16,128,128]{2,1,0:T(8,128)}, u32[]{:S(2)}) copy-start(f32[16,128,128]{2,1,0:T(8,128)} %get-tuple-element.28) | copy-start | bytes 3145732
  148.6 1.8 collective-permute-start.4
  155.8 3.6 %copy-start.5 = (f32[16,128,128]{2,1,0:T(8,128)S(1)}, f32[16,128,128]{2,1,0:T(8,128)}, u32[]{:S(2)}) copy-start(f32[16,128,128]{2,1,0:T(8,128)} %get-tuple-element.33) | copy-start | bytes 3145732
  155.8 3.6 %copy-start.8 = (f32[16,128,128]{1,2,0:T(8,128)S(1)}, f32[16,128,128]{1,2,0:T(8,128)}, u32[]{:S(2)}) copy-start(f32[16,128,128]{1,2,0:T(8,128)} %copy.67) | copy-start | bytes 3145732
  155.8 3.6 %copy-start.11 = (f32[16,128,128]{2,1,0:T(8,128)S(1)}, f32[16,128,128]{2,1,0:T(8,128)}, u32[]{:S(2)}) copy-start(f32[16,128,128]{2,1,0:T(8,128)} %get-tuple-element.27) | copy-start | bytes 3145732
  155.8 3.6 %copy-start.14 = (f32[16,128,128]{2,1,0:T(8,128)S(1)}, f32[16,128,128]{2,1,0:T(8,128)}, u32[]{:S(2)}) copy-start(f32[16,128,128]{2,1,0:T(8,128)} %get-tuple-element.28) | copy-start | bytes 3145732
  164.7 14.3 %all-to-all-start.2 = ((f32[128,1,8]{2,1,0:T(1,128)}), f32[128,1,8]{2,1,0:T(1,128)S(1)}, u32[]{:S(2)}, u32[]{:S(2)}) async-start(f32[128,1,8]{2,1,0:T(1,128)} %broadcast_in_dim.146), calls=%async_computation.2 | async-start | bytes 131072 | tf_op jit(solution)/shard_map/all_to_all | solution.py:150
  179.0 17.8 %all-to-all-start.3 = ((f32[16,16,256]{2,1,0:T(8,128)}), f32[16,16,256]{2,1,0:T(8,128)S(1)}, u32[]{:S(2)}, u32[]{:S(2)}) async-start(f32[16,16,256]{2,1,0:T(8,128)} %bitcast.44), calls=%async_computation.3 | async-start | bytes 524288 | tf_op jit(solution)/shard_map/all_to_all | solution.py:142
  196.8 2.1 %collective-permute-start.5 = (f32[8,16,256]{2,1,0:T(8,128)S(1)}, f32[8,16,256]{2,1,0:T(8,128)S(1)}, u32[]{:S(2)}, u32[]{:S(2)}) collective-permute-start(f32[8,16,256]{2,1,0:T(8,128)S(1)} %constant_dynamic-slice_fusion), channel_id=1, source_target_pairs={{0,16},{16,0},{1,17},{17,1},{2,18},{18,2},{3,19},{19,3},{4,20},{20... | collective-permute-start | bytes 393224 | tf_op jit(solution)/shard_map/ppermute | solution.py:145
Sparse Core Ops, SparseCore 0:
  13.6 52.6 all-gather.1
where the time goes:
time: 209 us; the launch traced here: 208 us
  waiting for transfers between devices  63.4 us (30%)
  other arithmetic  33 us (16%)
  between operations  31.8 us (15%)
  local copies, waits for them, and re-layouts  31.4 us (15%)
  starting transfers between devices  30 us (14%)
  matrix products  18 us (9%)
    all_gather x1, waiting for transfers between devices, local(): every = lax.all_gather(eight, 'y', axis=0, tiled=True)  34.8 us
    all_to_all x1, waiting for transfers between devices, local(): lax.all_to_all(jnp.take(every, left16, axis=0), COL, 0, 0, tiled=True)  16.2 us
    dot_general x3, matrix products, half_image(): middle = jnp.einsum('wjb,bi->wji', right, u, precision=high)  10.8 us
    all_to_all x1, waiting for transfers between devices, local(): lax.all_to_all(jnp.broadcast_to(mine_stats, (128, 8)), ALL, 0, 0, tiled=T...  8.72 us
    all_to_all x1, starting transfers between devices, local(): arrived = lax.all_to_all(slots, COL, 0, 0, tiled=True)  7.68 us
    dot_general x3, matrix products, half_image(): return jnp.einsum('wja,wai->ji', middle, left, precision=high)  7.13 us
    all_to_all x1, starting transfers between devices, local(): lax.all_to_all(jnp.take(every, left16, axis=0), COL, 0, 0, tiled=True)  6.71 us
    slice x3, local copies, waits for them, and re-layouts, unpack(): fold = packed[:, :HALF, :HALF]  5.98 us
  transfers between devices with their start and end apart: 11, of which 6 were waited for; matrix products, arithmetic and copies ran while one was open for 16% of the time, Pallas kernels for 0%

commit v1 on v0

--- a/solution.py
+++ b/solution.py
@@ -9,6 +9,11 @@
 ALL = ("y", "c", "x", "z")
 SWAP = [(0, 1), (1, 0)]
 high = lax.Precision.HIGH
+
+
+def gather_over(x, axis, dim):
+    sent = jnp.stack([x] * lax.axis_size(axis))
+    return jnp.concatenate(lax.all_to_all(sent, axis, 0, 0), axis=dim)
 
 
 def grids():
@@ -100,7 +105,7 @@
     mine = pack(lax.dynamic_index_in_dim(left_env, core, 1, keepdims=False))
     theirs = pack(lax.dynamic_index_in_dim(left_env, 1 - core, 1, keepdims=False))
     eight = in_order(core, mine, lax.ppermute(theirs, "c", SWAP))
-    every = lax.all_gather(eight, "y", axis=0, tiled=True)
+    every = gather_over(eight, "y", 0)
     right_term = lax.dynamic_index_in_dim(right_env, core, 1, keepdims=False)
     right_slots = pack(jnp.take(right_term, right16, axis=0) * on16[:, None, None])
     slots = jnp.concatenate([right_slots, thin16], axis=1)

time: 209 us -> 231 us (1.11)
  waiting for transfers between devices: 63.4 us -> 89.2 us
  between operations: 31.8 us -> 18.3 us
  starting transfers between devices: 30 us -> 37.2 us
  local copies, waits for them, and re-layouts: 31.4 us -> 34.2 us
    all_to_all x0 -> x1, waiting for transfers between devices: none -> 41.4 us  [gather_over(): return jnp.concatenate(lax.all_to_all(sent, axis, 0, 0), axis=dim)]
    all_gather x1 -> x0, waiting for transfers between devices: 34.8 us -> none  [local(): every = lax.all_gather(eight, 'y', axis=0, tiled=True)]
    all_to_all x1, waiting for transfers between devices: 0.01 us -> 22.7 us  [local(): arrived = lax.all_to_all(slots, COL, 0, 0, tiled=True)]
    all_to_all x0 -> x1, starting transfers between devices: none -> 5.02 us  [gather_over(): return jnp.concatenate(lax.all_to_all(sent, axis, 0, 0), axis=dim)]
    all_to_all x1, waiting for transfers between devices: 16.2 us -> 12.8 us  [local(): lax.all_to_all(jnp.take(every, left16, axis=0), COL, 0, 0, tiled=True)]
    ppermute x2, starting transfers between devices: 4.04 us -> 7.25 us  [operate(): return (part + lax.ppermute(part, 'c', SWAP)) * mask]
    another operation x1 -> x2, local copies, waits for them, and re-layouts: 0.01 us -> 2.48 us  [the longest x1 2.48 us: gather_over(): sent = jnp.stack([x] * lax.axis_size(axis))]
  transfers between devices with their start and end apart: 11 -> 11, of which waited for: 6 -> 7; matrix products, arithmetic and copies ran while one was open for 16% -> 14% of each run, Pallas kernels for 0% -> 0%
where the time goes in v1:
time: 231 us; the launch traced here: 229 us
  waiting for transfers between devices  89.2 us (39%)
  starting transfers between devices  37.2 us (16%)
  local copies, waits for them, and re-layouts  34.2 us (15%)
  other arithmetic  32.5 us (14%)
  between operations  18.3 us (8%)
  matrix products  18 us (8%)
    all_to_all x1, waiting for transfers between devices, gather_over(): return jnp.concatenate(lax.all_to_all(sent, axis, 0, 0), axis=dim)  41.4 us
    all_to_all x1, waiting for transfers between devices, local(): arrived = lax.all_to_all(slots, COL, 0, 0, tiled=True)  22.7 us
    all_to_all x1, waiting for transfers between devices, local(): lax.all_to_all(jnp.take(every, left16, axis=0), COL, 0, 0, tiled=True)  12.8 us
    dot_general x3, matrix products, half_image(): middle = jnp.einsum('wjb,bi->wji', right, u, precision=high)  10.8 us
    all_to_all x1, waiting for transfers between devices, local(): lax.all_to_all(jnp.broadcast_to(mine_stats, (128, 8)), ALL, 0, 0, tiled=T...  8.72 us
    all_to_all x1, starting transfers between devices, local(): arrived = lax.all_to_all(slots, COL, 0, 0, tiled=True)  7.58 us
    ppermute x2, starting transfers between devices, operate(): return (part + lax.ppermute(part, 'c', SWAP)) * mask  7.25 us
    dot_general x3, matrix products, half_image(): return jnp.einsum('wja,wai->ji', middle, left, precision=high)  7.21 us
  transfers between devices with their start and end apart: 11, of which 7 were waited for; matrix products, arithmetic and copies ran while one was open for 14% of the time, Pallas kernels for 0%

profile of v1, /device:TPU:1, one launch (start us, length us, event | category | flops | bytes accessed | tf_op | source)
XLA Modules:
  0.0 229.5 jit_solution(2158344535686885161)
XLA Ops:
  0.7 1.7 dynamic-slice_bitcast_fusion.1
  2.5 1.5 collective-permute-start.2
  4.0 1.6 collective-permute-done.2
  5.7 2.5 %stack.56 = f32[4,8,136,256]{3,2,1,0:T(8,128)} broadcast(f32[8,136,256]{2,1,0:T(8,128)S(1)} %maximum_select_fusion), dimensions={1,2,3} | broadcast | bytes 5570560 | tf_op jit(solution)/shard_map/stack | solution.py:15
  8.2 5.0 %all-to-all-start.1 = ((f32[4,8,136,256]{3,2,1,0:T(8,128)}), f32[4,8,136,256]{3,2,1,0:T(8,128)}, u32[]{:S(2)}, u32[]{:S(2)}) async-start(f32[4,8,136,256]{3,2,1,0:T(8,128)} %stack.56), calls=%async_computation.1 | async-start | bytes 8912896 | tf_op jit(solution)/shard_map/all_to_all | solution.py:16
  13.9 1.8 dynamic-slice_bitcast_fusion
  15.8 2.8 %gather_fusion = f32[16,256,256]{2,1,0:T(8,128)} fusion(f32[8,256,256]{2,1,0:T(8,128)S(1)} %dynamic-slice_bitcast_fusion, s32[1024]{0:T(1024)S(1)} %pad_clamp_fusion.3), kind=kCustom, calls=%fused_computation | custom fusion | bytes 8388672 | tf_op jit(solution)/shard_map/jit(_take)/gather | solution.py:110
  18.6 2.8 %select_multiply_fusion = f32[16,256,256]{2,1,0:T(8,128)S(1)} fusion(f32[16,256,256]{2,1,0:T(8,128)} %gather_fusion, f32[16]{0:T(128)S(1)} %get-tuple-element.64, pred[16]{0:T(512)(128)(4,1)S(1)} %and_bitcast_fusion), kind=kLoop, calls=%fused_computation.6 | loop fusion | flops 2097152 | bytes 8388688 | tf_op jit(solution)/shard_map/mul | solution.py:110
  21.7 1.7 fusion
  23.4 41.4 %all-to-all-done.1 = f32[4,8,136,256]{3,2,1,0:T(8,128)} async-done(((f32[4,8,136,256]{3,2,1,0:T(8,128)}), f32[4,8,136,256]{3,2,1,0:T(8,128)}, u32[]{:S(2)}, u32[]{:S(2)}) %all-to-all-start.1) | async-done | bytes 4456480 | tf_op jit(solution)/shard_map/all_to_all | solution.py:16
  64.8 7.6 %all-to-all-start = ((f32[16,152,256]{2,1,0:T(8,128)}), f32[16,152,256]{2,1,0:T(8,128)S(1)}, u32[]{:S(2)}, u32[]{:S(2)}) async-start(f32[16,152,256]{2,1,0:T(8,128)} %fusion), calls=%async_computation | async-start | bytes 4980736 | tf_op jit(solution)/shard_map/all_to_all | solution.py:112
  72.4 4.3 %gather_fusion.1 = f32[16,136,256]{2,1,0:T(8,128)} fusion(f32[32,136,256]{2,1,0:T(8,128)} %bitcast.22, s32[1024]{0:T(1024)S(1)} %pad_clamp_fusion.2), kind=kCustom, calls=%fused_computation.1 | custom fusion | bytes 4456512 | tf_op jit(solution)/shard_map/jit(_take)/gather | solution.py:115
  76.8 3.3 %broadcast_select_fusion = f32[16,136,256]{2,1,0:T(8,128)} fusion(f32[16,136,256]{2,1,0:T(8,128)} %gather_fusion.1, pred[16]{0:T(512)(128)(4,1)S(1)} %get-tuple-element.20), kind=kLoop, calls=%fused_computation.18 | loop fusion | flops 557056 | bytes 4456464 | tf_op jit(solution)/shard_map/jit(_take)/select_n | solution.py:115
  80.1 22.7 %all-to-all-done = f32[16,152,256]{2,1,0:T(8,128)S(1)} async-done(((f32[16,152,256]{2,1,0:T(8,128)}), f32[16,152,256]{2,1,0:T(8,128)S(1)}, u32[]{:S(2)}, u32[]{:S(2)}) %all-to-all-start) | async-done | bytes 2490400 | tf_op jit(solution)/shard_map/all_to_all | solution.py:112
  102.8 5.5 %all-to-all-start.2 = ((f32[16,136,256]{2,1,0:T(8,128)}), f32[16,136,256]{2,1,0:T(8,128)}, u32[]{:S(2)}, u32[]{:S(2)}) async-start(f32[16,136,256]{2,1,0:T(8,128)} %broadcast_select_fusion), calls=%async_computation.2 | async-start | bytes 4456448 | tf_op jit(solution)/shard_map/all_to_all | solution.py:115
  114.6 1.3 iota_compare_fusion.7
  116.5 0.7 multiply_reduce_fusion.7
  118.0 1.1 slice.189
  119.1 2.6 %copy.54 = f32[16,128,128]{1,2,0:T(8,128)} copy(f32[16,128,128]{2,1,0:T(8,128)} %slice.189) | data formatting | bytes 2097152 | tf_op jit(solution)/shard_map/slice | solution.py:38
  121.8 12.8 %all-to-all-done.2 = f32[16,136,256]{2,1,0:T(8,128)} async-done(((f32[16,136,256]{2,1,0:T(8,128)}), f32[16,136,256]{2,1,0:T(8,128)}, u32[]{:S(2)}, u32[]{:S(2)}) %all-to-all-start.2) | async-done | bytes 2228256 | tf_op jit(solution)/shard_map/all_to_all | solution.py:115
  134.6 2.3 %slice.198 = f32[16,128,128]{2,1,0:T(8,128)} slice(f32[16,136,256]{2,1,0:T(8,128)} %all-to-all-done.2), slice={[0:16], [0:128], [0:128]} | slice | bytes 2097152 | tf_op jit(solution)/shard_map/slice | solution.py:38
  136.9 2.6 %copy.66 = f32[16,128,128]{1,2,0:T(8,128)} copy(f32[16,128,128]{2,1,0:T(8,128)} %slice.198) | data formatting | bytes 2097152
  139.5 0.8 slice.200
  140.3 5.4 %bitcast_select_fusion.1 = (f32[16,128,128]{2,1,0:T(8,128)}, f32[16,128,128]{2,1,0:T(8,128)}, f32[16,128,128]{2,1,0:T(8,128)}, f32[16,128,128]{2,1,0:T(8,128)}, ...) fusion(f32[16,128,128]{1,2,0:T(8,128)} %copy.66, ...), kind=kLoop, calls=%fused_computation.21 | loop fusion | flops 1572864 | bytes 13697024 | tf_op jit(solution)/shard_map/jit(_where)/select_n | solution.py:42
  145.8 1.6 copy.56
  147.4 2.6 %copy.67 = f32[16,128,128]{1,2,0:T(8,128)} copy(f32[16,128,128]{2,1,0:T(8,128)} %get-tuple-element.33) | data formatting | bytes 2097152
  150.0 3.6 %fusion.7 = f32[16,256,256]{2,1,0:T(8,128)S(1)} fusion(f32[16,128,128]{2,1,0:T(8,128)} %get-tuple-element.46, f32[16,128,128]{2,1,0:T(8,128)S(1)} %copy.56, f32[16,128,128]{2,1,0:T(8,128)S(1)} %copy-done.2, f32[16,128,128]{2,1,0:T(8,128)} %get-tuple-element.47, f32[256,256]{1,0:T(8,128)S(1)} %fusion.10), kind=kOutput, calls=%fused_computation.31 | convolution fusion | flops 1613758464 | bytes 8650752 | tf_op jit(solution)/shard_map/wjb,bi->wji/dot_general | solution.py:123
  153.7 2.2 convolution_bitcast_fusion.2
  155.9 6.8 %collective-permute-start.3 = (f32[256,256]{1,0:T(8,128)S(1)}, f32[256,256]{1,0:T(8,128)S(1)}, u32[]{:S(2)}, u32[]{:S(2)}) collective-permute-start(f32[256,256]{1,0:T(8,128)S(1)} %convolution_bitcast_fusion.2), channel_id=1, source_target_pairs={{0,16},{16,0},{1,17},{17,1},{2,18},{18,2},{3,19},{19,3},{4,20},{20... | collective-permute-start | bytes 786440 | tf_op jit(solution)/shard_map/ppermute | solution.py:128
  162.7 1.1 collective-permute-done.3
  163.8 0.8 multiply_reduce_fusion.6
  164.6 1.5 multiply_reduce_fusion.5
  166.1 2.1 multiply_reduce_fusion.4
  168.8 1.5 divide_select_fusion.1
  170.3 3.6 %fusion.6 = f32[16,256,256]{2,1,0:T(8,128)S(1)} fusion(f32[16,128,128]{2,1,0:T(8,128)} %get-tuple-element.46, f32[16,128,128]{2,1,0:T(8,128)S(1)} %copy.56, f32[16,128,128]{2,1,0:T(8,128)S(1)} %copy-done.2, f32[16,128,128]{2,1,0:T(8,128)} %get-tuple-element.47, f32[256,256]{1,0:T(8,128)S(1)} %divide_select_fusion.1), kind=kOutput, calls=%fused_computation.30 | convolution fusion | flops 1613758464 | bytes 8650752 | tf_op jit(solution)/shard_map/wjb,bi->wji/dot_general | solution.py:123
  174.0 2.2 convolution_bitcast_fusion.1
  178.0 0.8 multiply_reduce_fusion.3
  178.8 1.6 multiply_reduce_fusion.2
  180.3 2.7 %multiply_reduce_fusion = (f32[]{:T(128)}, f32[256,256]{1,0:T(8,128)S(1)}) fusion(f32[]{:T(128)} %get-tuple-element.7, f32[256,256]{1,0:T(8,128)S(1)} %divide_select_fusion.1, f32[]{:T(128)} %get-tuple-element.6, f32[]{:T(128)} %sqrt.31, f32[256,256]{1,0:T(8,128)S(1)} %get-tuple-element.17, f32[]{:T(128)} %get-tuple-element.16, f32[]{:T(128)S(6)} %select_n.230, ...), kind=kLoop, calls=%fused_computation.47 | loop fusion | flops 917503 | bytes 1049113 | tf_op jit(solution)/shard_map/reduce_sum | solution.py:143
  183.8 3.6 %fusion.5 = f32[16,256,256]{2,1,0:T(8,128)S(1)} fusion(f32[16,128,128]{2,1,0:T(8,128)} %get-tuple-element.46, f32[16,128,128]{2,1,0:T(8,128)S(1)} %copy.56, f32[16,128,128]{2,1,0:T(8,128)S(1)} %copy-done.2, f32[16,128,128]{2,1,0:T(8,128)} %get-tuple-element.47, f32[256,256]{1,0:T(8,128)S(1)} %get-tuple-element.15, f32[]{:T(128)S(6)} %select_n.251, pred[]{:T(512)S(6)} %gt.28), kind=kOutput, calls=%fused_computation.29 | convolution fusion | flops 1613889536 | bytes 8650757 | tf_op jit(solution)/shard_map/wjb,bi->wji/dot_general | solution.py:123
  187.4 2.9 %fusion.8 = f32[]{:T(128)} fusion(f32[16,256,256]{2,1,0:T(8,128)S(1)} %fusion.5, f32[16,128,128]{2,1,0:T(8,128)S(1)} %copy-done.14, f32[16,128,128]{2,1,0:T(8,128)S(1)} %bitcast.179, f32[16,128,128]{2,1,0:T(8,128)S(1)} %copy-done.5, f32[16,128,128]{2,1,0:T(8,128)S(1)} %copy-done.11, f32[256,256]{1,0:T(8,128)S(1)} %get-tuple-element.15, f32[]{:T(128)S(6)} %select_n.251, ...), kind=kOutput, calls=%fused_computation.32 | convolution fusion | flops 1614020608 | bytes 8650761 | tf_op jit(solution)/shard_map/wja,wai->ji/dot_general | solution.py:124
  190.3 2.1 stack.62
  193.1 5.2 %all-to-all-start.3 = ((f32[128,1,8]{2,1,0:T(1,128)}), f32[128,1,8]{2,1,0:T(1,128)S(1)}, u32[]{:S(2)}, u32[]{:S(2)}) async-start(f32[128,1,8]{2,1,0:T(1,128)} %broadcast_in_dim.146), calls=%async_computation.3 | async-start | bytes 131072 | tf_op jit(solution)/shard_map/all_to_all | solution.py:155
  199.0 8.7 %all-to-all-done.3 = f32[128,1,8]{2,1,0:T(1,128)S(1)} async-done(((f32[128,1,8]{2,1,0:T(1,128)}), f32[128,1,8]{2,1,0:T(1,128)S(1)}, u32[]{:S(2)}, u32[]{:S(2)}) %all-to-all-start.3) | async-done | bytes 4128 | tf_op jit(solution)/shard_map/all_to_all | solution.py:155
  207.7 3.5 %all-to-all-start.4 = ((f32[16,16,256]{2,1,0:T(8,128)}), f32[16,16,256]{2,1,0:T(8,128)S(1)}, u32[]{:S(2)}, u32[]{:S(2)}) async-start(f32[16,16,256]{2,1,0:T(8,128)} %bitcast.45), calls=%async_computation.4 | async-start | bytes 524288 | tf_op jit(solution)/shard_map/all_to_all | solution.py:147
  225.5 1.1 collective-permute-start.5
  226.6 1.0 collective-permute-done.5
  227.6 0.8 add_bitcast_fusion
  (106 shorter events, 12.0 us)
Async XLA Ops:
  2.5 3.1 %collective-permute-start.2 = (f32[4,136,256]{2,1,0:T(8,128)S(1)}, f32[4,136,256]{2,1,0:T(8,128)S(1)}, u32[]{:S(2)}, u32[]{:S(2)}) collective-permute-start(f32[4,136,256]{2,1,0:T(8,128)S(1)} %select_maximum_fusion.1), channel_id=1, source_target_pairs={{0,16},{16,0},{1,17},{17,1},{2,18},{18,2},{3,19},{19,3},{4,20},{20... | collective-permute-start | bytes 1671176 | tf_op jit(solution)/shard_map/ppermute | solution.py:107
  8.2 5.0 %copy-start.16 = (s32[8,2]{0,1:T(2,128)S(1)}, s32[8,2]{0,1:T(2,128)}, u32[]{:S(2)}) copy-start(s32[8,2]{0,1:T(2,128)} %param.13) | copy-start | bytes 196
  8.2 5.0 %copy-start.17 = (s32[8]{0:T(128)S(1)}, s32[8]{0:T(128)}, u32[]{:S(2)}) copy-start(s32[8]{0:T(128)} %param.12) | copy-start | bytes 100
  8.2 5.5 %copy-start.15 = (f32[8,256,16]{1,2,0:T(8,128)S(1)}, f32[8,256,16]{1,2,0:T(8,128)}, u32[]{:S(2)}) copy-start(f32[8,256,16]{1,2,0:T(8,128)} %param.8) | copy-start | bytes 393220
  8.2 56.6 %all-to-all-start.1 = ((f32[4,8,136,256]{3,2,1,0:T(8,128)}), f32[4,8,136,256]{3,2,1,0:T(8,128)}, u32[]{:S(2)}, u32[]{:S(2)}) async-start(f32[4,8,136,256]{3,2,1,0:T(8,128)} %stack.56), calls=%async_computation.1 | async-start | bytes 8912896 | tf_op jit(solution)/shard_map/all_to_all | solution.py:16
  13.3 2.4 %collective-permute-start = (s32[8,3]{0,1:T(4,128)S(1)}, s32[8,3]{0,1:T(4,128)S(1)}, u32[]{:S(2)}, u32[]{:S(2)}) collective-permute-start(s32[8,3]{0,1:T(4,128)S(1)} %pad_add_fusion), channel_id=1, source_target_pairs={{0,16},{16,0},{1,17},{17,1},{2,18},{18,2},{3,19},{19,3},{4,20},{20... | collective-permute-start | bytes 296 | tf_op jit(solution)/shard_map/ppermute | solution.py:100
  13.7 7.9 %collective-permute-start.1 = (f32[8,16,256]{2,1,0:T(8,128)S(1)}, f32[8,16,256]{2,1,0:T(8,128)S(1)}, u32[]{:S(2)}, u32[]{:S(2)}) collective-permute-start(f32[8,16,256]{2,1,0:T(8,128)S(1)} %bitcast.180), channel_id=1, source_target_pairs={{0,16},{16,0},{1,17},{17,1},{2,18},{18,2},{3,19},{19,3},{4,20},{20... | collective-permute-start | bytes 393224 | tf_op jit(solution)/shard_map/ppermute | solution.py:101
  21.7 50.7 %copy-start.18 = (s32[64]{0:T(128)S(1)}, s32[64]{0:T(128)}, u32[]{:S(2)}) copy-start(s32[64]{0:T(128)} %param.11) | copy-start | bytes 772
  64.8 38.0 %all-to-all-start = ((f32[16,152,256]{2,1,0:T(8,128)}), f32[16,152,256]{2,1,0:T(8,128)S(1)}, u32[]{:S(2)}, u32[]{:S(2)}) async-start(f32[16,152,256]{2,1,0:T(8,128)} %fusion), calls=%async_computation | async-start | bytes 4980736 | tf_op jit(solution)/shard_map/all_to_all | solution.py:112
  76.8 34.1 %copy-start = (s32[32]{0:T(128)S(1)}, s32[32]{0:T(128)}, u32[]{:S(2)}) copy-start(s32[32]{0:T(128)} %param.14) | copy-start | bytes 388
  76.8 37.2 %copy-start.1 = (s32[8]{0:T(128)S(1)}, s32[8]{0:T(128)}, u32[]{:S(2)}) copy-start(s32[8]{0:T(128)} %param.15) | copy-start | bytes 100
  102.8 31.8 %all-to-all-start.2 = ((f32[16,136,256]{2,1,0:T(8,128)}), f32[16,136,256]{2,1,0:T(8,128)}, u32[]{:S(2)}, u32[]{:S(2)}) async-start(f32[16,136,256]{2,1,0:T(8,128)} %broadcast_select_fusion), calls=%async_computation.2 | async-start | bytes 4456448 | tf_op jit(solution)/shard_map/all_to_all | solution.py:115
  145.8 4.2 %copy-start.2 = (f32[16,128,128]{2,1,0:T(8,128)S(1)}, f32[16,128,128]{2,1,0:T(8,128)}, u32[]{:S(2)}) copy-start(f32[16,128,128]{2,1,0:T(8,128)} %get-tuple-element.44) | copy-start | bytes 3145732
  150.0 3.7 %copy-start.3 = (f32[16,128,128]{2,1,0:T(8,128)S(1)}, f32[16,128,128]{2,1,0:T(8,128)}, u32[]{:S(2)}) copy-start(f32[16,128,128]{2,1,0:T(8,128)} %get-tuple-element.33) | copy-start | bytes 3145732
  150.0 3.7 %copy-start.6 = (f32[16,128,128]{1,2,0:T(8,128)S(1)}, f32[16,128,128]{1,2,0:T(8,128)}, u32[]{:S(2)}) copy-start(f32[16,128,128]{1,2,0:T(8,128)} %copy.67) | copy-start | bytes 3145732
  150.0 3.7 %copy-start.9 = (f32[16,128,128]{2,1,0:T(8,128)S(1)}, f32[16,128,128]{2,1,0:T(8,128)}, u32[]{:S(2)}) copy-start(f32[16,128,128]{2,1,0:T(8,128)} %get-tuple-element.27) | copy-start | bytes 3145732
  150.0 3.7 %copy-start.12 = (f32[16,128,128]{2,1,0:T(8,128)S(1)}, f32[16,128,128]{2,1,0:T(8,128)}, u32[]{:S(2)}) copy-start(f32[16,128,128]{2,1,0:T(8,128)} %get-tuple-element.28) | copy-start | bytes 3145732
  155.9 8.0 %collective-permute-start.3 = (f32[256,256]{1,0:T(8,128)S(1)}, f32[256,256]{1,0:T(8,128)S(1)}, u32[]{:S(2)}, u32[]{:S(2)}) collective-permute-start(f32[256,256]{1,0:T(8,128)S(1)} %convolution_bitcast_fusion.2), channel_id=1, source_target_pairs={{0,16},{16,0},{1,17},{17,1},{2,18},{18,2},{3,19},{19,3},{4,20},{20... | collective-permute-start | bytes 786440 | tf_op jit(solution)/shard_map/ppermute | solution.py:128
  170.3 3.7 %copy-start.4 = (f32[16,128,128]{2,1,0:T(8,128)S(1)}, f32[16,128,128]{2,1,0:T(8,128)}, u32[]{:S(2)}) copy-start(f32[16,128,128]{2,1,0:T(8,128)} %get-tuple-element.33) | copy-start | bytes 3145732
  170.3 3.7 %copy-start.7 = (f32[16,128,128]{1,2,0:T(8,128)S(1)}, f32[16,128,128]{1,2,0:T(8,128)}, u32[]{:S(2)}) copy-start(f32[16,128,128]{1,2,0:T(8,128)} %copy.67) | copy-start | bytes 3145732
  170.3 3.7 %copy-start.10 = (f32[16,128,128]{2,1,0:T(8,128)S(1)}, f32[16,128,128]{2,1,0:T(8,128)}, u32[]{:S(2)}) copy-start(f32[16,128,128]{2,1,0:T(8,128)} %get-tuple-element.27) | copy-start | bytes 3145732
  170.3 3.7 %copy-start.13 = (f32[16,128,128]{2,1,0:T(8,128)S(1)}, f32[16,128,128]{2,1,0:T(8,128)}, u32[]{:S(2)}) copy-start(f32[16,128,128]{2,1,0:T(8,128)} %get-tuple-element.28) | copy-start | bytes 3145732
  176.2 1.8 collective-permute-start.4
  183.8 3.6 %copy-start.5 = (f32[16,128,128]{2,1,0:T(8,128)S(1)}, f32[16,128,128]{2,1,0:T(8,128)}, u32[]{:S(2)}) copy-start(f32[16,128,128]{2,1,0:T(8,128)} %get-tuple-element.33) | copy-start | bytes 3145732
  183.8 3.6 %copy-start.8 = (f32[16,128,128]{1,2,0:T(8,128)S(1)}, f32[16,128,128]{1,2,0:T(8,128)}, u32[]{:S(2)}) copy-start(f32[16,128,128]{1,2,0:T(8,128)} %copy.67) | copy-start | bytes 3145732
  183.8 3.6 %copy-start.11 = (f32[16,128,128]{2,1,0:T(8,128)S(1)}, f32[16,128,128]{2,1,0:T(8,128)}, u32[]{:S(2)}) copy-start(f32[16,128,128]{2,1,0:T(8,128)} %get-tuple-element.27) | copy-start | bytes 3145732
  183.8 3.6 %copy-start.14 = (f32[16,128,128]{2,1,0:T(8,128)S(1)}, f32[16,128,128]{2,1,0:T(8,128)}, u32[]{:S(2)}) copy-start(f32[16,128,128]{2,1,0:T(8,128)} %get-tuple-element.28) | copy-start | bytes 3145732
  193.1 14.6 %all-to-all-start.3 = ((f32[128,1,8]{2,1,0:T(1,128)}), f32[128,1,8]{2,1,0:T(1,128)S(1)}, u32[]{:S(2)}, u32[]{:S(2)}) async-start(f32[128,1,8]{2,1,0:T(1,128)} %broadcast_in_dim.146), calls=%async_computation.3 | async-start | bytes 131072 | tf_op jit(solution)/shard_map/all_to_all | solution.py:155
  207.7 17.8 %all-to-all-start.4 = ((f32[16,16,256]{2,1,0:T(8,128)}), f32[16,16,256]{2,1,0:T(8,128)S(1)}, u32[]{:S(2)}, u32[]{:S(2)}) async-start(f32[16,16,256]{2,1,0:T(8,128)} %bitcast.45), calls=%async_computation.4 | async-start | bytes 524288 | tf_op jit(solution)/shard_map/all_to_all | solution.py:147
  225.5 2.1 collective-permute-start.5
